TPU v7x, 128 devices: a whole 4x4x4 slice. The times are simulated.
128 devices in a mesh: gen: 4 (over z), learn: 32 (over x, y, core).
Axes of the slice: x: 4, y: 4, z: 4, core: 2. Of those that a mesh axis runs over, the one named last changes fastest.
Arguments:
- hidden: bfloat16 [32768, 5120], P(('gen', 'learn')), may hold values from -0.59765625 to 0.59765625
- cotangent: bfloat16 [32768, 1024], P(('gen', 'learn')), may hold values from -0.29882812 to 0.29882812
- importance: float32 [32768], P(('gen', 'learn')), may hold values from 0.25 to 4
- block_len: int32 [4096], P(('gen', 'learn')), may hold values from 1 to 8
- version: int32 [4096], P(('gen', 'learn')), may hold values from 0 to 3
- destination: int32 [4096, 1], P(('gen', 'learn')), may hold values from 0 to 31; in each aligned block of 32 rows (0 to 31, 32 to 63, ...) at most 2 rows name the same one
- w_key: bfloat16 [5120, 1024], replicated, may hold values from -0.078125 to 0.078125
- in_gain: float32 [5120], replicated, may hold values from 0.5 to 1.5
- key_gain: float32 [128], replicated, may hold values from 0.5 to 1.5
Outputs:
- grad_slots: bfloat16 [65536, 5120], P(('gen', 'learn'))
- w_grad: float32 [5120, 1024], P('gen')
- gain_grad: float32 [5120], replicated
- kgain_grad: float32 [128], replicated
Inputs may be any that keep to these rules, and one draw needn't show every extreme that they name: `destination`: the 32 blocks of one device name each learner at most 2 times.
All inputs are finite; a program needn't handle non-finite values.
Results may differ from a plain program's by a relative error of at most 0.0075.
Values may be sent and summed in bfloat16 or wider, within the bound.
A program may use at most 128 MiB of HBM per device.

v0:
```python
import jax
import jax.numpy as jnp
from jax import lax
from jax.sharding import PartitionSpec as P

TILE = 8
VERSIONS = 4
SLOTS = 64
epsilon = 1e-06
clip_ratio = 2.0
staleness = 0.5


def packed_total(arrays, axis):
    ends = [0]
    for a in arrays:
        ends.append(ends[-1] + a.size)
    so_far = lax.psum(jnp.concatenate([a.ravel() for a in arrays]), axis)
    return tuple((so_far[b:e].reshape(a.shape) for a, b, e in zip(arrays, ends, ends[1:])))


def token_weights(importance, block_len, version):
    tile_count = block_len.shape[0]
    inside = (lax.broadcasted_iota(jnp.int32, (tile_count, TILE), 1) < block_len[:, None]).astype(
        jnp.float32
    )
    stale_age = (VERSIONS - 1 - version).astype(jnp.float32)
    decay_factor = jnp.power(jnp.float32(staleness), stale_age)
    return jnp.minimum(importance, clip_ratio) * (decay_factor[:, None] * inside).reshape(-1)


def layer_pass(hidden, upstream_rows, w_key, in_gain, key_gain):
    row_count = hidden.shape[0]
    x_float = hidden.astype(jnp.float32)
    inv_rms = lax.rsqrt(jnp.mean(x_float * x_float, -1, keepdims=True) + epsilon)
    normed = x_float * inv_rms
    h_rows = (normed * in_gain).astype(jnp.bfloat16)
    key_rows = jnp.dot(h_rows, w_key, preferred_element_type=jnp.float32).reshape(
        row_count, -1, key_gain.shape[0]
    )
    key_scale = lax.rsqrt(jnp.mean(key_rows * key_rows, -1, keepdims=True) + epsilon)
    upstream = upstream_rows.astype(jnp.float32).reshape(key_rows.shape)
    kgain_part = jnp.sum(upstream * key_rows * key_scale, axis=(0, 1))
    scaled = upstream * key_gain
    grad_keys = key_scale * scaled - key_rows * key_scale**3 * jnp.mean(
        scaled * key_rows, -1, keepdims=True
    )
    grad_keys = grad_keys.reshape(row_count, -1).astype(jnp.bfloat16)
    grad_h = lax.dot_general(
        grad_keys, w_key, (((1,), (1,)), ((), ())), preferred_element_type=jnp.float32
    )
    gain_part = jnp.sum(grad_h * normed, 0)
    grad_normed = grad_h * in_gain
    grad_input = inv_rms * (
        grad_normed - normed * jnp.mean(grad_normed * normed, -1, keepdims=True)
    )
    return (grad_input.astype(jnp.bfloat16), h_rows, grad_keys, gain_part, kgain_part)


def body(hidden, cotangent, importance, block_len, version, destination, w_key, in_gain, key_gain):
    learners = lax.axis_size("learn")
    generators = lax.axis_size("gen")
    capacity = SLOTS // learners
    tile_count = block_len.shape[0]
    model_width = hidden.shape[1]
    weights = token_weights(importance, block_len, version)
    upstream_all = (cotangent.astype(jnp.float32) * weights[:, None]).astype(jnp.bfloat16)
    dest_column = destination[:, 0]
    onehot = (dest_column[:, None] == jnp.arange(learners, dtype=jnp.int32)[None, :]).astype(
        jnp.int32
    )
    slot_rank = jnp.sum((jnp.cumsum(onehot, 0) - onehot) * onehot, 1)
    target = dest_column * capacity + slot_rank
    placing = (target[None, :] == jnp.arange(SLOTS, dtype=jnp.int32)[:, None]).astype(jnp.bfloat16)
    grad_local, h_rows, grad_keys, gain_part, kgain_part = layer_pass(
        hidden, upstream_all, w_key, in_gain, key_gain
    )
    feature_count = grad_local.shape[1]
    spread = jnp.dot(
        placing,
        grad_local.reshape(tile_count, TILE * feature_count),
        preferred_element_type=jnp.float32,
    )
    grad_slots = lax.all_to_all(
        spread.astype(jnp.bfloat16).reshape(SLOTS * TILE, feature_count),
        "learn",
        split_axis=0,
        concat_axis=0,
        tiled=True,
    )
    row_count = h_rows.shape[0]
    group_width = model_width // generators
    sliced = h_rows.reshape(row_count, generators, group_width)
    arrived_rows = lax.all_to_all(sliced, "gen", split_axis=1, concat_axis=0, tiled=True).reshape(
        generators * row_count, group_width
    )
    gathered_keys = lax.all_gather(grad_keys, "gen", axis=0, tiled=True)
    partial_rows = lax.dot_general(
        arrived_rows, gathered_keys, (((0,), (0,)), ((), ())), preferred_element_type=jnp.float32
    )
    w_grad = lax.psum(partial_rows, "learn")
    gain_grad, kgain_grad = packed_total((gain_part, kgain_part), ("gen", "learn"))
    return (grad_slots, w_grad, gain_grad, kgain_grad)


def solution(mesh):
    return jax.shard_map(
        body,
        mesh=mesh,
        in_specs=(
            P(("gen", "learn"), None),
            P(("gen", "learn"), None),
            P(("gen", "learn")),
            P(("gen", "learn")),
            P(("gen", "learn")),
            P(("gen", "learn"), None),
            P(),
            P(),
            P(),
        ),
        out_specs=(P(("gen", "learn"), None), P("gen", None), P(), P()),
        check_vma=False,
    )
```

profile of v0, /device:TPU:1, one launch (start us, length us, event | category | flops | bytes accessed | tf_op | source)
XLA Modules:
  0.0 262.8 jit_solution(8460036367396275193)
XLA Ops:
  7.2 2.3 fusion.10
  9.6 2.5 fusion.4
  12.1 6.5 %fusion.19 = f32[256,1024]{1,0:T(8,128)S(1)} fusion(bf16[256,5120]{1,0:T(8,128)(2,1)S(1)} %fusion.4, bf16[5120,1024]{1,0:T(8,128)(2,1)} %param.15), kind=kOutput, calls=%fused_computation.47 | convolution fusion | flops 2684354560 | bytes 14155776 | tf_op jit(solution)/shard_map/dot_general | solution.py:38
  19.6 0.7 multiply_reduce_fusion.1
  20.9 0.3 mul.155
  21.2 0.3 mul.168
  21.5 0.3 mul.174
  21.9 1.8 fusion.15
  23.8 3.6 %copy.36 = bf16[32,4,8,1280]{3,2,0,1:T(8,128)(2,1)} copy(bf16[32,4,8,1280]{3,2,1,0:T(8,128)(2,1)} %bitcast.43) | data formatting | bytes 5242880 | tf_op jit(solution)/shard_map/reshape | solution.py:93
  27.3 5.8 %all-to-all-start.1 = ((bf16[256,4,1280]{2,0,1:T(8,128)(2,1)}), bf16[256,4,1280]{2,0,1:T(8,128)(2,1)}, u32[]{:S(2)}, u32[]{:S(2)}) async-start(bf16[256,4,1280]{2,0,1:T(8,128)(2,1)} %bitcast.44), calls=%async_computation.1 | async-start | bytes 5242880 | tf_op jit(solution)/shard_map/all_to_all | solution.py:94
  33.2 6.5 %fusion.9 = (f32[5120]{0:T(1024)S(1)}, f32[256]{0:T(256)S(1)}, f32[256,5120]{1,0:T(8,128)S(1)}) fusion(bf16[256,5120]{1,0:T(8,128)(2,1)S(1)} %copy-done, f32[256]{0:T(256)S(1)} %add_rsqrt_fusion.1, f32[5120]{0:T(1024)S(1)} %copy-done.5, bf16[256,1024]{1,0:T(8,128)(2,1)S(1)} %copy-done.3, bf16[5120,1024]{1,0:T(8,128)(2,1)} %param.15), kind=kOutput, calls=%fused_computation.12 | convolution fusion | flops 2693524224 | bytes 18917376 | tf_op jit(solution)/shard_map/dot_general | solution.py:49
  39.7 3.0 %fusion.8 = bf16[256,5120]{1,0:T(8,128)(2,1)} fusion(bf16[256,5120]{1,0:T(8,128)(2,1)S(1)} %copy-done, f32[256,5120]{1,0:T(8,128)S(1)} %get-tuple-element.12, f32[256]{0:T(256)S(1)} %broadcast_multiply_fusion.1, f32[5120]{0:T(1024)S(1)} %copy-done.5, f32[256]{0:T(256)S(1)} %add_rsqrt_fusion.1), kind=kLoop, calls=%fused_computation.11 | loop fusion | flops 9175040 | bytes 10508288 | tf_op jit(solution)/shard_map/convert_element_type | solution.py:57
  42.7 3.2 %reshape.87 = bf16[32,40960]{1,0:T(8,128)(2,1)S(1)} reshape(bf16[256,5120]{1,0:T(8,128)(2,1)} %fusion.8) | data formatting | bytes 5242880 | tf_op jit(solution)/shard_map/reshape | solution.py:81
  46.2 3.9 %convolution_convert_fusion = bf16[64,40960]{1,0:T(8,128)(2,1)} fusion(bf16[32,40960]{1,0:T(8,128)(2,1)S(1)} %reshape.87, s32[32]{0:T(128)S(1)} %multiply_add_fusion), kind=kOutput, calls=%fused_computation | convolution fusion | flops 170395648 | bytes 7864448 | tf_op jit(solution)/shard_map/dot_general | solution.py:79
  50.1 8.1 %all_to_all.19 = bf16[32,16,5120]{2,1,0:T(8,128)(2,1)} reshape(bf16[64,40960]{1,0:T(8,128)(2,1)} %convolution_convert_fusion) | data formatting | bytes 10485760 | tf_op jit(solution)/shard_map/all_to_all | solution.py:84
  58.2 23.3 %all-to-all-done.1 = bf16[256,4,1280]{2,0,1:T(8,128)(2,1)} async-done(((bf16[256,4,1280]{2,0,1:T(8,128)(2,1)}), bf16[256,4,1280]{2,0,1:T(8,128)(2,1)}, u32[]{:S(2)}, u32[]{:S(2)}) %all-to-all-start.1) | async-done | bytes 2621472 | tf_op jit(solution)/shard_map/all_to_all | solution.py:94
  81.5 8.8 %all-to-all-start = ((bf16[32,16,5120]{2,1,0:T(8,128)(2,1)}), bf16[32,16,5120]{2,1,0:T(8,128)(2,1)}, u32[]{:S(2)}, u32[]{:S(2)}) async-start(bf16[32,16,5120]{2,1,0:T(8,128)(2,1)} %all_to_all.19), calls=%async_computation | async-start | bytes 10485760 | tf_op jit(solution)/shard_map/all_to_all | solution.py:84
  90.4 7.7 %fusion.20 = f32[1280,1024]{1,0:T(8,128)} fusion(bf16[1024,1280]{1,0:T(8,128)(2,1)} %bitcast.5, bf16[1024,1024]{1,0:T(8,128)(2,1)} %all-gather.2.cloned.1.call-done), kind=kOutput, calls=%fused_computation.48 | convolution fusion | flops 2684354560 | bytes 9961472 | tf_op jit(solution)/shard_map/dot_general | solution.py:98
  98.1 120.7 %psum.15 = f32[5248]{0:T(1024)S(1)} all-reduce(f32[5248]{0:T(1024)S(1)} %pad_maximum_fusion), channel_id=1, replica_groups=mesh['gen'=4,'learn'=32] {'gen','learn'}, use_global_device_ids=true, to_apply=%region_10.11 | all-reduce | flops 5248 | bytes 41984 | tf_op jit(solution)/shard_map/psum | solution.py:18
  218.8 0.6 slice.8
  219.4 0.5 slice.9
  219.9 28.3 %all-reduce.2.cloned.1.call-done = f32[1280,1024]{1,0:T(8,128)} async-done(((f32[1280,1024]{1,0:T(8,128)}), f32[1280,1024]{1,0:T(8,128)}) %all-reduce.2.cloned.1.call-update) | async-done | bytes 5242896 | tf_op jit(solution)/shard_map/psum | solution.py:101
  248.2 5.3 %copy.39 = bf16[512,5120]{1,0:T(8,128)(2,1)} copy(bf16[512,5120]{1,0:T(8,128)(2,1)} %bitcast.2) | data formatting | bytes 10485760
  253.6 2.4 copy.40
  (52 shorter events, 1.9 us)
Async XLA Ops:
  7.2 83.2 %all-gather.2.cloned.1.call-start = ((), (), s32[]{:S(2)}) async-start(), calls=%async_computation.2 | async-start | bytes 2621440 | tf_op jit(solution)/shard_map/all_gather | solution.py:97
  12.1 6.6 %copy-start.1 = (bf16[256,5120]{1,0:T(8,128)(2,1)}, bf16[256,5120]{1,0:T(8,128)(2,1)S(1)}, u32[]{:S(2)}) copy-start(bf16[256,5120]{1,0:T(8,128)(2,1)S(1)} %fusion.4) | copy-start | bytes 7864324
  12.1 6.8 %copy-start.10 = (s32[32]{0:T(128)S(1)}, s32[32]{0:T(128)}, u32[]{:S(2)}) copy-start(s32[32]{0:T(128)} %param.13) | copy-start | bytes 388
  12.1 6.8 %copy-start.9 = (s32[32]{0:T(128)S(1)}, s32[32]{0:T(128)}, u32[]{:S(2)}) copy-start(s32[32]{0:T(128)} %param.12) | copy-start | bytes 388
  12.1 7.0 %copy-start.8 = (f32[256]{0:T(256)S(1)}, f32[256]{0:T(256)}, u32[]{:S(2)}) copy-start(f32[256]{0:T(256)} %param.11) | copy-start | bytes 3076
  12.1 7.0 %copy-start.4 = (bf16[256,1024]{1,0:T(8,128)(2,1)S(1)}, bf16[256,1024]{1,0:T(8,128)(2,1)}, u32[]{:S(2)}) copy-start(bf16[256,1024]{1,0:T(8,128)(2,1)} %param.10) | copy-start | bytes 1572868
  18.7 0.8 copy-start.6
  23.7 9.4 %copy-start = (bf16[256,5120]{1,0:T(8,128)(2,1)S(1)}, bf16[256,5120]{1,0:T(8,128)(2,1)}, u32[]{:S(2)}) copy-start(bf16[256,5120]{1,0:T(8,128)(2,1)} %param.9) | copy-start | bytes 7864324
  23.8 9.4 %copy-start.3 = (bf16[256,1024]{1,0:T(8,128)(2,1)S(1)}, bf16[256,1024]{1,0:T(8,128)(2,1)}, u32[]{:S(2)}) copy-start(bf16[256,1024]{1,0:T(8,128)(2,1)} %get-tuple-element.9) | copy-start | bytes 1572868
  23.8 9.4 %copy-start.5 = (f32[5120]{0:T(1024)S(1)}, f32[5120]{0:T(1024)}, u32[]{:S(2)}) copy-start(f32[5120]{0:T(1024)} %param.16) | copy-start | bytes 61444
  27.3 54.1 %all-to-all-start.1 = ((bf16[256,4,1280]{2,0,1:T(8,128)(2,1)}), bf16[256,4,1280]{2,0,1:T(8,128)(2,1)}, u32[]{:S(2)}, u32[]{:S(2)}) async-start(bf16[256,4,1280]{2,0,1:T(8,128)(2,1)} %bitcast.44), calls=%async_computation.1 | async-start | bytes 5242880 | tf_op jit(solution)/shard_map/all_to_all | solution.py:94
  42.7 3.2 %copy-start.7 = (s32[32,1]{0,1:T(1,128)S(1)}, s32[32,1]{0,1:T(1,128)}, u32[]{:S(2)}) copy-start(s32[32,1]{0,1:T(1,128)} %param.14) | copy-start | bytes 388
  81.5 138.5 %all-to-all-start = ((bf16[32,16,5120]{2,1,0:T(8,128)(2,1)}), bf16[32,16,5120]{2,1,0:T(8,128)(2,1)}, u32[]{:S(2)}, u32[]{:S(2)}) async-start(bf16[32,16,5120]{2,1,0:T(8,128)(2,1)} %all_to_all.19), calls=%async_computation | async-start | bytes 10485760 | tf_op jit(solution)/shard_map/all_to_all | solution.py:84
  90.3 157.9 %all-reduce.2.cloned.1.call-start = ((), (), s32[]{:S(2)}) async-start(), calls=%async_computation.3 | async-start | bytes 10485760 | tf_op jit(solution)/shard_map/psum | solution.py:101
  248.2 5.3 %copy-start.2 = (f32[1280,1024]{1,0:T(8,128)S(1)}, f32[1280,1024]{1,0:T(8,128)}, u32[]{:S(2)}) copy-start(f32[1280,1024]{1,0:T(8,128)} %all-reduce.2.cloned.1.call-done) | copy-start | bytes 15728644
Sparse Core Ops, SparseCore 0:
  23.9 59.1 all-gather.1
  98.2 149.9 all-reduce.1
where the time goes:
time: 263 us
  blocking collectives  121 us (46%)
  waiting for transfers between devices  51.6 us (20%)
  local copies, waits for them, and re-layouts  25.7 us (10%)
  matrix products  24.5 us (9%)
  starting transfers between devices  14.8 us (6%)
  between operations  14.3 us (5%)
  other arithmetic  11.1 us (4%)
    psum x1, blocking collectives, packed_total(): so_far = lax.psum(jnp.concatenate([a.ravel() for a in arrays]), axis)  121 us
    psum x1, waiting for transfers between devices, body(): w_grad = lax.psum(partial_rows, 'learn')  28.3 us
    all_to_all x1, waiting for transfers between devices, body(): lax.all_to_all(sliced, 'gen', split_axis=1, concat_axis=0, tiled=True)  23.3 us
    all_to_all x1, starting transfers between devices, body(): lax.all_to_all(spread.astype(jnp.bfloat16).reshape(SLOTS * TILE, feature_...  8.84 us
    unnamed x26, local copies, waits for them, and re-layouts  8.15 us
    all_to_all x1, local copies, waits for them, and re-layouts, body(): lax.all_to_all(spread.astype(jnp.bfloat16).reshape(SLOTS * TILE, feature_...  8.08 us
    dot_general x1, matrix products, body(): lax.dot_general(arrived_rows, gathered_keys, (((0,), (0,)), ((), ())), pr...  7.66 us
    dot_general x1, matrix products, layer_pass(): jnp.dot(h_rows, w_key, preferred_element_type=jnp.float32)  6.55 us
  transfers between devices with their start and end apart: 4, of which 2 were waited for; matrix products, arithmetic and copies ran while one was open for 11% of the time, Pallas kernels for 0%

commit v1 on v0

--- a/solution.py
+++ b/solution.py
@@ -98,7 +98,9 @@
     partial_rows = lax.dot_general(
         arrived_rows, gathered_keys, (((0,), (0,)), ((), ())), preferred_element_type=jnp.float32
     )
-    w_grad = lax.psum(partial_rows, "learn")
+    w_grad = partial_rows
+    for hop in (1, 2, 4, 8, 16):
+        w_grad = w_grad + lax.ppermute(w_grad, "learn", [(dev, dev ^ hop) for dev in range(32)])
     gain_grad, kgain_grad = packed_total((gain_part, kgain_part), ("gen", "learn"))
     return (grad_slots, w_grad, gain_grad, kgain_grad)
 

time: 263 us -> 709 us (2.70)
  waiting for transfers between devices: 51.6 us -> 333 us
  blocking collectives: 121 us -> 263 us
  other arithmetic: 11.1 us -> 37.3 us
    ppermute x0 -> x5, waiting for transfers between devices: none -> 332 us  [body(): lax.ppermute(w_grad, 'learn', [(dev, dev ^ hop) for dev in range(32)])]
    psum x1, blocking collectives: 121 us -> 209 us  [packed_total(): so_far = lax.psum(jnp.concatenate([a.ravel() for a in arrays]), axis)]
    all_to_all x0 -> x1, blocking collectives: none -> 53.7 us  [body(): lax.all_to_all(sliced, 'gen', split_axis=1, concat_axis=0, tiled=True)]
    psum x1 -> x0, waiting for transfers between devices: 28.3 us -> none  [body(): w_grad = lax.psum(partial_rows, 'learn')]
    add x0 -> x5, other arithmetic: none -> 23.4 us  [body(): w_grad + lax.ppermute(w_grad, 'learn', [(dev, dev ^ hop) for dev in range...]
    all_to_all x1 -> x0, waiting for transfers between devices: 23.3 us -> none  [body(): lax.all_to_all(sliced, 'gen', split_axis=1, concat_axis=0, tiled=True)]
    ppermute x0 -> x5, starting transfers between devices: none -> 9.48 us  [body(): lax.ppermute(w_grad, 'learn', [(dev, dev ^ hop) for dev in range(32)])]
  transfers between devices with their start and end apart: 4 -> 7, of which waited for: 2 -> 5; matrix products, arithmetic and copies ran while one was open for 11% -> 3% of each run, Pallas kernels for 0% -> 0%
where the time goes in v1:
time: 709 us; the launch traced here: 708 us
  waiting for transfers between devices  333 us (47%)
  blocking collectives  263 us (37%)
  other arithmetic  37.3 us (5%)
  local copies, waits for them, and re-layouts  24 us (3%)
  matrix products  18.5 us (3%)
  starting transfers between devices  18 us (3%)
  between operations  14.3 us (2%)
    ppermute x5, waiting for transfers between devices, body(): lax.ppermute(w_grad, 'learn', [(dev, dev ^ hop) for dev in range(32)])  332 us
    psum x1, blocking collectives, packed_total(): so_far = lax.psum(jnp.concatenate([a.ravel() for a in arrays]), axis)  209 us
    all_to_all x1, blocking collectives, body(): lax.all_to_all(sliced, 'gen', split_axis=1, concat_axis=0, tiled=True)  53.7 us
    add x5, other arithmetic, body(): w_grad + lax.ppermute(w_grad, 'learn', [(dev, dev ^ hop) for dev in range...  23.4 us
  transfers between devices with their start and end apart: 7, of which 5 were waited for; matrix products, arithmetic and copies ran while one was open for 3% of the time, Pallas kernels for 0%

profile of v1, /device:TPU:1, one launch (start us, length us, event | category | flops | bytes accessed | tf_op | source)
XLA Modules:
  0.0 707.9 jit_solution(10041885584375264945)
XLA Ops:
  8.1 2.3 fusion.10
  16.7 2.9 fusion.19
  22.2 3.1 fusion.15
  25.3 1.9 copy.36
  27.2 53.7 %all_to_all.27 = bf16[256,4,1280]{2,0,1:T(8,128)(2,1)} all-to-all(bf16[256,4,1280]{2,0,1:T(8,128)(2,1)S(1)} %bitcast.44), channel_id=1, replica_groups=mesh['gen'=4,'learn'=32] {'gen'}, dimensions={1} | all-to-all | bytes 5242880 | tf_op jit(solution)/shard_map/all_to_all | solution.py:94
  81.8 5.3 fusion.20
  88.1 8.3 %collective-permute-done = f32[1280,1024]{1,0:T(8,128)S(1)} collective-permute-done((f32[1280,1024]{1,0:T(8,128)S(1)}, f32[1280,1024]{1,0:T(8,128)S(1)}, u32[]{:S(2)}, u32[]{:S(2)}) %collective-permute-start) | collective-permute-done | bytes 5242912 | tf_op jit(solution)/shard_map/ppermute | solution.py:103
  99.7 112.9 %collective-permute-done.1 = f32[1280,1024]{1,0:T(8,128)S(1)} collective-permute-done((f32[1280,1024]{1,0:T(8,128)S(1)}, f32[1280,1024]{1,0:T(8,128)S(1)}, u32[]{:S(2)}, u32[]{:S(2)}) %collective-permute-start.1) | collective-permute-done | bytes 5242912 | tf_op jit(solution)/shard_map/ppermute | solution.py:103
  212.6 1.8 add.55
  214.4 3.0 collective-permute-start.2
  217.4 112.0 %collective-permute-done.2 = f32[1280,1024]{1,0:T(8,128)S(1)} collective-permute-done((f32[1280,1024]{1,0:T(8,128)S(1)}, f32[1280,1024]{1,0:T(8,128)S(1)}, u32[]{:S(2)}, u32[]{:S(2)}) %collective-permute-start.2) | collective-permute-done | bytes 5242912 | tf_op jit(solution)/shard_map/ppermute | solution.py:103
  329.4 3.6 add.56
  334.2 6.5 fusion.9
  340.6 3.0 fusion.8
  343.7 3.2 reshape.87
  347.2 98.6 %collective-permute-done.3 = f32[1280,1024]{1,0:T(8,128)} collective-permute-done((f32[1280,1024]{1,0:T(8,128)}, f32[1280,1024]{1,0:T(8,128)}, u32[]{:S(2)}, u32[]{:S(2)}) %collective-permute-start.3) | collective-permute-done | bytes 5242912 | tf_op jit(solution)/shard_map/ppermute | solution.py:103
  445.8 8.1 %add.57 = f32[1280,1024]{1,0:T(8,128)} add(f32[1280,1024]{1,0:T(8,128)} %add.56, f32[1280,1024]{1,0:T(8,128)} %collective-permute-done.3) | non-fusion elementwise | flops 1310720 | bytes 15728640 | tf_op jit(solution)/shard_map/add | solution.py:103
  453.9 2.7 collective-permute-start.4
  456.7 3.9 convolution_convert_fusion
  460.5 8.1 %all_to_all.19 = bf16[32,16,5120]{2,1,0:T(8,128)(2,1)} reshape(bf16[64,40960]{1,0:T(8,128)(2,1)} %convolution_convert_fusion) | data formatting | bytes 10485760 | tf_op jit(solution)/shard_map/all_to_all | solution.py:84
  468.6 8.5 %all-to-all-start = ((bf16[32,16,5120]{2,1,0:T(8,128)(2,1)}), bf16[32,16,5120]{2,1,0:T(8,128)(2,1)}, u32[]{:S(2)}, u32[]{:S(2)}) async-start(bf16[32,16,5120]{2,1,0:T(8,128)(2,1)} %all_to_all.19), calls=%async_computation | async-start | bytes 10485760 | tf_op jit(solution)/shard_map/all_to_all | solution.py:84
  477.1 209.5 %psum.7 = f32[5248]{0:T(1024)S(1)} all-reduce(f32[5248]{0:T(1024)S(1)} %pad_maximum_fusion), channel_id=1, replica_groups=mesh['gen'=4,'learn'=32] {'gen','learn'}, use_global_device_ids=true, to_apply=%region_9.10 | all-reduce | flops 5248 | bytes 41984 | tf_op jit(solution)/shard_map/psum | solution.py:18
  687.7 8.2 %add.58 = f32[1280,1024]{1,0:T(8,128)} add(f32[1280,1024]{1,0:T(8,128)} %add.57, f32[1280,1024]{1,0:T(8,128)} %collective-permute-done.4) | non-fusion elementwise | flops 1310720 | bytes 15728640 | tf_op jit(solution)/shard_map/add | solution.py:103
  695.9 5.2 copy.38
  (64 shorter events, 17.5 us)
Async XLA Ops:
  7.2 7.1 copy-start
  7.2 7.0 copy-start.9
  7.2 7.0 copy-start.5
  7.2 74.6 %all-gather.2.cloned.1.call-start = ((), (), s32[]{:S(2)}) async-start(), calls=%async_computation.2 | async-start | bytes 2621440 | tf_op jit(solution)/shard_map/all_gather | solution.py:97
  10.4 4.6 copy-start.7
  12.6 4.1 copy-start.11
  16.7 2.9 copy-start.1
  19.6 1.0 copy-start.2
  19.6 2.5 copy-start.4
  87.1 9.3 %collective-permute-start = (f32[1280,1024]{1,0:T(8,128)S(1)}, f32[1280,1024]{1,0:T(8,128)S(1)}, u32[]{:S(2)}, u32[]{:S(2)}) collective-permute-start(f32[1280,1024]{1,0:T(8,128)S(1)} %fusion.20), channel_id=1, source_target_pairs={{0,1},{1,0},{2,3},{3,2},{4,5},{5,4},{6,7},{7,6},{8,9},{9,8},{10,11... | collective-permute-start | bytes 15728648 | tf_op jit(solution)/shard_map/ppermute | solution.py:103
  98.1 114.5 %collective-permute-start.1 = (f32[1280,1024]{1,0:T(8,128)S(1)}, f32[1280,1024]{1,0:T(8,128)S(1)}, u32[]{:S(2)}, u32[]{:S(2)}) collective-permute-start(f32[1280,1024]{1,0:T(8,128)S(1)} %add.54), channel_id=1, source_target_pairs={{0,2},{1,3},{2,0},{3,1},{4,6},{5,7},{6,4},{7,5},{8,10},{9,11},{10,... | collective-permute-start | bytes 15728648 | tf_op jit(solution)/shard_map/ppermute | solution.py:103
  214.4 119.8 %copy-start.3 = (bf16[256,1024]{1,0:T(8,128)(2,1)S(1)}, bf16[256,1024]{1,0:T(8,128)(2,1)}, u32[]{:S(2)}) copy-start(bf16[256,1024]{1,0:T(8,128)(2,1)} %get-tuple-element.9) | copy-start | bytes 1572868
  214.4 119.8 %copy-start.6 = (f32[5120]{0:T(1024)S(1)}, f32[5120]{0:T(1024)}, u32[]{:S(2)}) copy-start(f32[5120]{0:T(1024)} %param.16) | copy-start | bytes 61444
  214.4 119.7 %copy-start.8 = (f32[256]{0:T(256)S(1)}, f32[256]{0:T(256)}, u32[]{:S(2)}) copy-start(f32[256]{0:T(256)} %copy-done.7) | copy-start | bytes 3076
  214.4 115.0 %collective-permute-start.2 = (f32[1280,1024]{1,0:T(8,128)S(1)}, f32[1280,1024]{1,0:T(8,128)S(1)}, u32[]{:S(2)}, u32[]{:S(2)}) collective-permute-start(f32[1280,1024]{1,0:T(8,128)S(1)} %add.55), channel_id=1, source_target_pairs={{0,4},{1,5},{2,6},{3,7},{4,0},{5,1},{6,2},{7,3},{8,12},{9,13},{10,... | collective-permute-start | bytes 15728648 | tf_op jit(solution)/shard_map/ppermute | solution.py:103
  332.9 112.8 %collective-permute-start.3 = (f32[1280,1024]{1,0:T(8,128)}, f32[1280,1024]{1,0:T(8,128)}, u32[]{:S(2)}, u32[]{:S(2)}) collective-permute-start(f32[1280,1024]{1,0:T(8,128)} %add.56), channel_id=1, source_target_pairs={{0,8},{1,9},{2,10},{3,11},{4,12},{5,13},{6,14},{7,15},{8,0},{9,1},... | collective-permute-start | bytes 15728648 | tf_op jit(solution)/shard_map/ppermute | solution.py:103
  343.7 3.2 copy-start.10
  453.9 233.8 %collective-permute-start.4 = (f32[1280,1024]{1,0:T(8,128)}, f32[1280,1024]{1,0:T(8,128)}, u32[]{:S(2)}, u32[]{:S(2)}) collective-permute-start(f32[1280,1024]{1,0:T(8,128)} %add.57), channel_id=1, source_target_pairs={{0,16},{1,17},{2,18},{3,19},{4,20},{5,21},{6,22},{7,23},{8,24},{9,... | collective-permute-start | bytes 15728648 | tf_op jit(solution)/shard_map/ppermute | solution.py:103
  468.6 219.1 %all-to-all-start = ((bf16[32,16,5120]{2,1,0:T(8,128)(2,1)}), bf16[32,16,5120]{2,1,0:T(8,128)(2,1)}, u32[]{:S(2)}, u32[]{:S(2)}) async-start(bf16[32,16,5120]{2,1,0:T(8,128)(2,1)} %all_to_all.19), calls=%async_computation | async-start | bytes 10485760 | tf_op jit(solution)/shard_map/all_to_all | solution.py:84
Sparse Core Ops, SparseCore 0:
  25.4 56.3 all-gather.1
